TPU v7x, 512 devices: a whole 4x8x8 slice. The times are simulated.
512 devices in a mesh: axial: 64 (over x, z, core), radial: 8 (over y).
Axes of the slice: x: 4, y: 8, z: 8, core: 2. Of those that a mesh axis runs over, the one named last changes fastest.
Arguments:
- state_start: float32 [5, 640, 128, 128], P(None, 'axial', 'radial'), may hold values from -6 to 6
- forcing: float32 [640, 128, 128], P('axial', 'radial'), may hold values from -6 to 6
- signal: float32 [8], replicated, may hold values from -1 to 1
- mixing: float32 [2, 5, 5], replicated, may hold values from -0.4 to 0.4
- panel_cell: int32 [64, 8, 64, 4], P('axial', 'radial'), may hold values from -1 to 20479, as said below
- amplitude: float32 [64, 8, 64, 4, 512], P('axial', 'radial'), may hold values from -0.015625 to 0.015625
- delay: float32 [64, 8, 64, 4, 512], P('axial', 'radial'), may hold values from 0 to 8
- observer_list: int32 [512], replicated, may hold values from 0 to 511, each once
Outputs:
- final_state: float32 [5, 640, 128, 128], P(None, 'axial', 'radial')
- spectra: float32 [2, 4, 512], P(None, None, ('axial', 'radial'))
- adjoint_state: float32 [5, 640, 128, 128], P(None, 'axial', 'radial')
- forcing_grad: float32 [640, 128, 128], P('axial', 'radial')
Inputs may be any that keep to these rules, and one draw needn't show every extreme that they name: `panel_cell`: each entry is a cell index of the sending tile, of 20480 cells, or -1 for an empty slot; the live slots of one tile and owner come first; one owner in each draw receives 4 live slots from every tile, and the largest cell index is reached.
All inputs are finite; a program needn't handle non-finite values.
Results may differ from a plain program's by a relative error of at most 0.0003.
Values sent between devices are 32-bit elements; how exact they have to be, the bound alone decides.
A program may use at most 128 MiB of HBM per device.

v0:
```python
import math

import jax
import jax.numpy as jnp
from jax import lax
from jax.sharding import PartitionSpec as P

STEPS = 8
FREQ = 4


deriv_coef = (5.0 / 6.0, -5.0 / 21.0, 5.0 / 84.0, -5.0 / 504.0, 1.0 / 1260.0)
filter_coef = tuple(
    ((-1.0) ** abs(offset) * math.comb(10, 5 + offset) / 1024.0 for offset in range(-5, 6))
)
damping = 0.2
highest = lax.Precision.HIGHEST


def extended(block, sides, width):
    for axis, dim in sides:
        count = lax.axis_size(axis)
        forward = [(i, i + 1) for i in range(count - 1)]
        backward = [(target, source) for source, target in forward]
        low = lax.ppermute(
            lax.slice_in_dim(block, block.shape[dim] - width, None, axis=dim), axis, forward
        )
        high = lax.ppermute(lax.slice_in_dim(block, 0, width, axis=dim), axis, backward)
        block = jnp.concatenate([low, block, high], axis=dim)
    return block


def advance(padded, mixing, adjoint):
    span_x = padded.shape[1] - 10
    span_r = padded.shape[2] - 10
    count = padded.shape[0]

    def along_x(offset):
        return padded[:, 5 + offset : 5 + offset + span_x, 5 : 5 + span_r, :]

    def along_r(offset):
        return padded[:, 5 : 5 + span_x, 5 + offset : 5 + offset + span_r, :]

    centre = along_x(0)
    deriv_x = sum(
        (deriv_coef[order] * (along_x(order + 1) - along_x(-order - 1)) for order in range(5))
    )
    deriv_r = sum(
        (deriv_coef[order] * (along_r(order + 1) - along_r(-order - 1)) for order in range(5))
    )
    smooth = sum(
        (filter_coef[offset + 5] * (along_x(offset) + along_r(offset)) for offset in range(-5, 6))
    )
    factor = 1.0 if adjoint else -1.0
    outputs = []
    for target in range(count):
        term = centre[target] - damping * smooth[target]
        for source in range(count):
            if adjoint:
                coef_x = mixing[0, source, target]
                coef_r = mixing[1, source, target]
            else:
                coef_x = mixing[0, target, source]
                coef_r = mixing[1, target, source]
            term = term + factor * (coef_x * deriv_x[source] + coef_r * deriv_r[source])
        outputs.append(term)
    return jnp.stack(outputs)


def frequencies():
    return 2.0 * jnp.pi * (jnp.arange(FREQ, dtype=jnp.float32) + 1.0) / STEPS


def time_tables():
    levels = jnp.arange(STEPS, dtype=jnp.float32)
    phase = levels[:, None] * frequencies()[None, :]
    return (jnp.cos(phase), jnp.sin(phase))


def panel_kernels(amp, lag):
    phase = frequencies()[None, :, None] * lag[:, None, :]
    return (amp[:, None, :] * jnp.cos(phase), -amp[:, None, :] * jnp.sin(phase))


def partial_spectra(panels, kern_re, kern_im, cos_t, sin_t):
    coef_re = jnp.dot(panels, cos_t, precision=highest)
    coef_im = -jnp.dot(panels, sin_t, precision=highest)
    spec_re = jnp.einsum("pfo,pf->fo", kern_re, coef_re, precision=highest) - jnp.einsum(
        "pfo,pf->fo", kern_im, coef_im, precision=highest
    )
    spec_im = jnp.einsum("pfo,pf->fo", kern_re, coef_im, precision=highest) + jnp.einsum(
        "pfo,pf->fo", kern_im, coef_re, precision=highest
    )
    return jnp.stack([spec_re, spec_im])


def panel_sources(spectra, kern_re, kern_im, cos_t, sin_t):
    back_re = jnp.einsum("pfo,fo->pf", kern_re, spectra[0], precision=highest) + jnp.einsum(
        "pfo,fo->pf", kern_im, spectra[1], precision=highest
    )
    back_im = jnp.einsum("pfo,fo->pf", kern_im, spectra[0], precision=highest) - jnp.einsum(
        "pfo,fo->pf", kern_re, spectra[1], precision=highest
    )
    return 2.0 * (
        jnp.dot(back_re, cos_t.T, precision=highest) + jnp.dot(back_im, sin_t.T, precision=highest)
    )


def on_device(state_start, forcing, signal, mixing, panel_cell, amplitude, delay, observer_list):
    slots = panel_cell[0, 0]
    cell_total = forcing.shape[0] * forcing.shape[1] * forcing.shape[2]
    live = slots >= 0
    targets = jnp.where(live, slots, cell_total)
    clipped = jnp.minimum(targets, cell_total - 1)
    state = state_start
    records = []
    for level in range(STEPS):
        padded = extended(state, (("axial", 1), ("radial", 2)), 5)
        state = advance(padded, mixing, False).at[4].add(signal[level] * forcing)
        records.append(jnp.where(live, jnp.take(state[4].reshape(-1), clipped), 0.0))
    stacked = jnp.stack(records, axis=-1)
    received = lax.all_to_all(stacked, "axial", split_axis=0, concat_axis=0, tiled=True)
    observers = observer_list.shape[0]
    chosen_amp = jnp.take(amplitude[0, 0], observer_list, axis=2).reshape(-1, observers)
    chosen_lag = jnp.take(delay[0, 0], observer_list, axis=2).reshape(-1, observers)
    kern_re, kern_im = panel_kernels(chosen_amp, chosen_lag)
    cos_t, sin_t = time_tables()
    partial_sum = partial_spectra(received.reshape(-1, STEPS), kern_re, kern_im, cos_t, sin_t)
    share = observers // lax.axis_size(("axial", "radial"))
    total = lax.psum(partial_sum, ("axial", "radial"))
    mine = lax.dynamic_slice_in_dim(total, lax.axis_index(("axial", "radial")) * share, share, 2)
    sources = panel_sources(total, kern_re, kern_im, cos_t, sin_t).reshape(received.shape)
    returned = lax.all_to_all(sources, "axial", split_axis=0, concat_axis=0, tiled=True)
    flat_targets = targets.reshape(-1)
    adjoint = jnp.zeros_like(state_start)
    gradient = jnp.zeros_like(forcing)
    for level in reversed(range(STEPS)):
        spread = (
            jnp.zeros((cell_total,), jnp.float32)
            .at[flat_targets]
            .add(returned[:, :, level].reshape(-1), mode="drop")
        )
        carried = adjoint.at[4].add(spread.reshape(forcing.shape))
        gradient = gradient + signal[level] * carried[4]
        padded = extended(carried, (("axial", 1), ("radial", 2)), 5)
        adjoint = advance(padded, mixing, True)
    return (state, mine, adjoint, gradient)


def solution(mesh):
    return jax.shard_map(
        on_device,
        mesh=mesh,
        in_specs=(
            P(None, "axial", "radial", None),
            P("axial", "radial", None),
            P(),
            P(),
            P("axial", "radial", None, None),
            P("axial", "radial", None, None, None),
            P("axial", "radial", None, None, None),
            P(),
        ),
        out_specs=(
            P(None, "axial", "radial", None),
            P(None, None, ("axial", "radial")),
            P(None, "axial", "radial", None),
            P("axial", "radial", None),
        ),
        check_vma=False,
    )
```

profile of v0, /device:TPU:1, one launch (start us, length us, event | category | flops | bytes accessed | tf_op | source)
XLA Modules:
  0.0 1145.6 jit_solution(15424200699040122054)
XLA Ops:
  23.6 6.8 collective-permute-done.3
  46.2 6.4 constant_dynamic-update-slice_fusion.9
  103.9 6.5 constant_dynamic-update-slice_fusion.14
  163.3 6.4 constant_dynamic-update-slice_fusion.19
  203.1 6.6 collective-permute-done.14
  228.1 6.4 constant_dynamic-update-slice_fusion.24
  293.4 6.4 constant_dynamic-update-slice_fusion.29
  312.9 6.6 collective-permute-start.20
  355.0 6.4 constant_dynamic-update-slice_fusion.34
  414.0 6.4 constant_dynamic-update-slice_fusion.39
  472.9 6.4 constant_dynamic-update-slice_fusion.44
  497.8 20.8 %all-to-all-start = ((f32[64,4,8]{2,1,0:T(4,128)}), f32[64,4,8]{2,1,0:T(4,128)S(1)}, u32[]{:S(2)}, u32[]{:S(2)}) async-start(f32[64,4,8]{2,1,0:T(4,128)} %copy.48), calls=%async_computation | async-start | bytes 262144 | tf_op jit(solution)/shard_map/all_to_all | solution.py:122
  518.6 17.0 %fusion = (f32[256,4,512]{2,1,0:T(4,128)}, f32[256,4,512]{2,1,0:T(4,128)}) fusion(f32[256,512]{1,0:T(8,128)S(1)} %mul.7300, f32[4]{0:T(128)S(1)} %add_multiply_fusion, f32[256,512]{1,0:T(8,128)S(1)} %mul.7297, f32[256,512]{1,0:T(8,128)S(1)} %neg.11), kind=kLoop, calls=%fused_computation.28 | loop fusion | flops 1572864 | bytes 5767184 | tf_op jit(solution)/shard_map/mul | solution.py:82
  548.8 97.6 %psum.7 = f32[2,4,512]{2,1,0:T(4,128)S(1)} all-reduce(f32[2,4,512]{2,1,0:T(4,128)S(1)} %pad_maximum_fusion.62), channel_id=1, replica_groups=mesh['axial'=64,'radial'=8] {'axial','radial'}, use_global_device_ids=true, to_apply=%region_0.3 | all-reduce | flops 4096 | bytes 32768 | tf_op jit(solution)/shard_map/psum | solution.py:130
  654.0 6.9 all-to-all-start.1
  660.9 10.3 all-to-all-done.1
  710.7 6.5 constant_dynamic-update-slice_fusion.57
  770.0 6.5 constant_dynamic-update-slice_fusion.62
  776.5 6.4 constant_dynamic-update-slice_fusion.61
  829.9 6.5 constant_dynamic-update-slice_fusion.67
  836.4 6.4 constant_dynamic-update-slice_fusion.66
  888.9 6.5 constant_dynamic-update-slice_fusion.72
  895.4 6.4 constant_dynamic-update-slice_fusion.71
  946.8 6.5 constant_dynamic-update-slice_fusion.77
  953.3 6.4 constant_dynamic-update-slice_fusion.76
  1004.3 6.5 constant_dynamic-update-slice_fusion.82
  1010.8 6.4 constant_dynamic-update-slice_fusion.81
  1062.0 6.5 constant_dynamic-update-slice_fusion.87
  1068.5 6.4 constant_dynamic-update-slice_fusion.86
  1074.9 11.2 bitcast_add_fusion
  1125.6 6.5 constant_dynamic-update-slice_fusion.92
  1132.2 6.4 constant_dynamic-update-slice_fusion.91
  (424 shorter events, 810.3 us)
Async XLA Ops:
  1.8 15.4 %collective-permute-start = (f32[5,5,16,128]{3,2,1,0:T(8,128)S(1)}, f32[5,5,16,128]{3,2,1,0:T(8,128)S(1)}, u32[]{:S(2)}, u32[]{:S(2)}) collective-permute-start(f32[5,5,16,128]{3,2,1,0:T(8,128)S(1)} %get-tuple-element.372), channel_id=1, source_target_pairs={{0,8},{8,16},{16,24},{24,32},{32,40},{40,48},{48,56},{56,64},{64,7... | collective-permute-start | bytes 614408 | tf_op jit(solution)/shard_map/ppermute | solution.py:25
  7.2 10.2 collective-permute-start.1
  17.4 13.1 %collective-permute-start.3 = (f32[5,20,5,128]{3,2,1,0:T(8,128)S(1)}, f32[5,20,5,128]{3,2,1,0:T(8,128)S(1)}, u32[]{:S(2)}, u32[]{:S(2)}) collective-permute-start(f32[5,20,5,128]{3,2,1,0:T(8,128)S(1)} %get-tuple-element.337), channel_id=1, source_target_pairs={{1,0},{2,1},{3,2},{4,3},{5,4},{6,5},{7,6},{9,8},{10,9},{11,10},{12... | collective-permute-start | bytes 768008 | tf_op jit(solution)/shard_map/ppermute | solution.py:28
  18.7 13.1 %collective-permute-start.2 = (f32[5,20,5,128]{3,2,1,0:T(8,128)S(1)}, f32[5,20,5,128]{3,2,1,0:T(8,128)S(1)}, u32[]{:S(2)}, u32[]{:S(2)}) collective-permute-start(f32[5,20,5,128]{3,2,1,0:T(8,128)S(1)} %get-tuple-element.338), channel_id=1, source_target_pairs={{0,1},{1,2},{2,3},{3,4},{4,5},{5,6},{6,7},{8,9},{9,10},{10,11},{11... | collective-permute-start | bytes 768008 | tf_op jit(solution)/shard_map/ppermute | solution.py:25
  75.0 10.6 collective-permute-start.6
  79.1 10.6 collective-permute-start.7
  137.8 11.5 %collective-permute-start.11 = (f32[5,20,5,128]{3,2,1,0:T(8,128)S(1)}, f32[5,20,5,128]{3,2,1,0:T(8,128)S(1)}, u32[]{:S(2)}, u32[]{:S(2)}) collective-permute-start(f32[5,20,5,128]{3,2,1,0:T(8,128)S(1)} %get-tuple-element.332), channel_id=1, source_target_pairs={{1,0},{2,1},{3,2},{4,3},{5,4},{6,5},{7,6},{9,8},{10,9},{11,10},{12... | collective-permute-start | bytes 768008 | tf_op jit(solution)/shard_map/ppermute | solution.py:28
  183.8 12.3 %collective-permute-start.12 = (f32[5,5,16,128]{3,2,1,0:T(8,128)}, f32[5,5,16,128]{3,2,1,0:T(8,128)S(1)}, u32[]{:S(2)}, u32[]{:S(2)}) collective-permute-start(f32[5,5,16,128]{3,2,1,0:T(8,128)} %get-tuple-element.363), channel_id=1, source_target_pairs={{0,8},{8,16},{16,24},{24,32},{32,40},{40,48},{48,56},{56,64},{64,7... | collective-permute-start | bytes 614408 | tf_op jit(solution)/shard_map/ppermute | solution.py:25
  186.8 9.2 collective-permute-start.13
  196.2 13.6 %collective-permute-start.14 = (f32[5,20,5,128]{3,2,1,0:T(8,128)S(1)}, f32[5,20,5,128]{3,2,1,0:T(8,128)S(1)}, u32[]{:S(2)}, u32[]{:S(2)}) collective-permute-start(f32[5,20,5,128]{3,2,1,0:T(8,128)S(1)} %get-tuple-element.327), channel_id=1, source_target_pairs={{0,1},{1,2},{2,3},{3,4},{4,5},{5,6},{6,7},{8,9},{9,10},{10,11},{11... | collective-permute-start | bytes 768008 | tf_op jit(solution)/shard_map/ppermute | solution.py:25
  201.4 12.6 %collective-permute-start.15 = (f32[5,20,5,128]{3,2,1,0:T(8,128)S(1)}, f32[5,20,5,128]{3,2,1,0:T(8,128)S(1)}, u32[]{:S(2)}, u32[]{:S(2)}) collective-permute-start(f32[5,20,5,128]{3,2,1,0:T(8,128)S(1)} %get-tuple-element.328), channel_id=1, source_target_pairs={{1,0},{2,1},{3,2},{4,3},{5,4},{6,5},{7,6},{9,8},{10,9},{11,10},{12... | collective-permute-start | bytes 768008 | tf_op jit(solution)/shard_map/ppermute | solution.py:28
  248.6 13.4 %collective-permute-start.16 = (f32[5,5,16,128]{3,2,1,0:T(8,128)}, f32[5,5,16,128]{3,2,1,0:T(8,128)S(1)}, u32[]{:S(2)}, u32[]{:S(2)}) collective-permute-start(f32[5,5,16,128]{3,2,1,0:T(8,128)} %get-tuple-element.361), channel_id=1, source_target_pairs={{0,8},{8,16},{16,24},{24,32},{32,40},{40,48},{48,56},{56,64},{64,7... | collective-permute-start | bytes 614408 | tf_op jit(solution)/shard_map/ppermute | solution.py:25
  262.8 10.7 collective-permute-start.18
  267.5 10.7 collective-permute-start.19
  312.9 11.0 collective-permute-start.20
  329.7 10.2 collective-permute-start.23
  389.4 9.4 collective-permute-start.27
  433.5 9.8 collective-permute-start.28
  497.8 42.9 %all-to-all-start = ((f32[64,4,8]{2,1,0:T(4,128)}), f32[64,4,8]{2,1,0:T(4,128)S(1)}, u32[]{:S(2)}, u32[]{:S(2)}) async-start(f32[64,4,8]{2,1,0:T(4,128)} %copy.48), calls=%async_computation | async-start | bytes 262144 | tf_op jit(solution)/shard_map/all_to_all | solution.py:122
  654.0 17.2 %all-to-all-start.1 = ((f32[64,4,8]{2,1,0:T(4,128)}), f32[64,4,8]{2,1,0:T(4,128)S(1)}, u32[]{:S(2)}, u32[]{:S(2)}) async-start(f32[64,4,8]{2,1,0:T(4,128)} %bitcast.105), calls=%async_computation.1 | async-start | bytes 262144 | tf_op jit(solution)/shard_map/all_to_all | solution.py:133
  686.7 10.1 collective-permute-start.35
  743.0 9.0 collective-permute-start.38
  746.0 10.1 collective-permute-start.39
  802.4 9.5 collective-permute-start.42
  805.9 10.1 collective-permute-start.43
  861.6 9.4 collective-permute-start.46
  864.9 10.1 collective-permute-start.47
  919.6 9.2 collective-permute-start.50
  922.8 10.1 collective-permute-start.51
  980.3 10.1 collective-permute-start.55
  1038.0 10.1 collective-permute-start.59
  1101.7 10.1 collective-permute-start.63
  (46 other events, 365.9 us)
where the time goes:
time: 1160 us; the launch traced here: 1150 us
  other arithmetic  585 us (50%)
  starting transfers between devices  209 us (18%)
  waiting for transfers between devices  186 us (16%)
  blocking collectives  97.6 us (8%)
  local copies, waits for them, and re-layouts  49.8 us (4%)
  matrix products  14.5 us (1%)
    unnamed x71, other arithmetic  411 us
    ppermute x32, starting transfers between devices, extended(): lax.ppermute(lax.slice_in_dim(block, block.shape[dim] - width, None, axis...  126 us
    ppermute x32, waiting for transfers between devices, extended(): lax.ppermute(lax.slice_in_dim(block, 0, width, axis=dim), axis, backward)  124 us
    psum x1, blocking collectives, on_device(): total = lax.psum(partial_sum, ('axial', 'radial'))  97.6 us
    another operation x15, other arithmetic, advance(): return jnp.stack(outputs)  92.6 us
    ppermute x32, starting transfers between devices, extended(): lax.ppermute(lax.slice_in_dim(block, 0, width, axis=dim), axis, backward)  55.2 us
    ppermute x32, waiting for transfers between devices, extended(): lax.ppermute(lax.slice_in_dim(block, block.shape[dim] - width, None, axis...  51.9 us
  transfers between devices with their start and end apart: 66, of which 55 were waited for; matrix products, arithmetic and copies ran while one was open for 7% of the time, Pallas kernels for 0%

commit v1 on v0

--- a/solution.py
+++ b/solution.py
@@ -1,8 +1,11 @@
+import functools
 import math
 
 import jax
 import jax.numpy as jnp
 from jax import lax
+from jax.experimental import pallas as pl
+from jax.experimental.pallas import tpu as pltpu
 from jax.sharding import PartitionSpec as P
 
 STEPS = 8
@@ -67,6 +70,98 @@
     return jnp.stack(outputs)
 
 
+HALO = 5
+
+
+def neighbour_halos(block):
+    axial = lax.axis_size("axial")
+    radial = lax.axis_size("radial")
+    up_a = [(i, i + 1) for i in range(axial - 1)]
+    down_a = [(i + 1, i) for i in range(axial - 1)]
+    up_r = [(i, i + 1) for i in range(radial - 1)]
+    down_r = [(i + 1, i) for i in range(radial - 1)]
+    rows = block.shape[1]
+    cols = block.shape[2]
+    x_low = lax.ppermute(block[:, rows - HALO :], "axial", up_a)
+    x_high = lax.ppermute(block[:, :HALO], "axial", down_a)
+    r_low = lax.ppermute(block[:, :, cols - HALO :], "radial", up_r)
+    r_high = lax.ppermute(block[:, :, :HALO], "radial", down_r)
+    return x_low, x_high, r_low, r_high
+
+
+def step_kernel(with_extra, coef, block, x_low, x_high, r_low, r_high, *rest):
+    if with_extra:
+        extra, out, ext_r = rest
+    else:
+        out, ext_r = rest
+    count, rows, cols, _ = block.shape
+    top = 8
+    for s in range(count):
+        ext_r[s, :, top - HALO : top, :] = r_low[s]
+        ext_r[s, :, top : top + cols, :] = block[s]
+        ext_r[s, :, top + cols : top + cols + HALO, :] = r_high[s]
+    cx = [[coef[t * count + s] for s in range(count)] for t in range(count)]
+    cr = [[coef[count * count + t * count + s] for s in range(count)] for t in range(count)]
+    for i in range(rows):
+        acc = [None] * count
+        for s in range(count):
+
+            def along_x(k):
+                j = i + k
+                if j < 0:
+                    return x_low[s, HALO + j]
+                if j >= rows:
+                    return x_high[s, j - rows]
+                return block[s, j]
+
+            def along_r(k):
+                return ext_r[s, i, top + k : top + k + cols, :]
+
+            centre = block[s, i]
+            dx = None
+            dr = None
+            smooth = filter_coef[HALO] * (centre + centre)
+            for o in range(1, HALO + 1):
+                xp, xm = along_x(o), along_x(-o)
+                rp, rm = along_r(o), along_r(-o)
+                tx = deriv_coef[o - 1] * (xp - xm)
+                tr = deriv_coef[o - 1] * (rp - rm)
+                dx = tx if dx is None else dx + tx
+                dr = tr if dr is None else dr + tr
+                smooth = smooth + filter_coef[HALO + o] * ((xp + xm) + (rp + rm))
+            for t in range(count):
+                term = cx[t][s] * dx + cr[t][s] * dr
+                if t == s:
+                    term = term + (centre - damping * smooth)
+                acc[t] = term if acc[t] is None else acc[t] + term
+        for t in range(count):
+            value = acc[t]
+            if with_extra and t == count - 1:
+                value = value + coef[2 * count * count] * extra[i]
+            out[t, i] = value
+
+
+def stencil_step(block, mixing_x, mixing_r, scale=None, extra=None):
+    count, rows, cols, lanes = block.shape
+    halos = neighbour_halos(block)
+    with_extra = extra is not None
+    pieces = [mixing_x.reshape(-1), mixing_r.reshape(-1)]
+    if with_extra:
+        pieces.append(jnp.reshape(scale, (1,)))
+    coef = jnp.concatenate(pieces)
+    args = [coef, block, *halos] + ([extra] if with_extra else [])
+    vmem = pl.BlockSpec(memory_space=pltpu.VMEM)
+    cells = count * rows * cols * lanes
+    return pl.pallas_call(
+        functools.partial(step_kernel, with_extra),
+        out_shape=jax.ShapeDtypeStruct(block.shape, jnp.float32),
+        in_specs=[pl.BlockSpec(memory_space=pltpu.SMEM)] + [vmem] * (len(args) - 1),
+        out_specs=vmem,
+        scratch_shapes=[pltpu.VMEM((count, rows, cols + 16, lanes), jnp.float32)],
+        cost_estimate=pl.CostEstimate(flops=80 * cells, bytes_accessed=16 * cells, transcendentals=0),
+    )(*args)
+
+
 def frequencies():
     return 2.0 * jnp.pi * (jnp.arange(FREQ, dtype=jnp.float32) + 1.0) / STEPS
 
@@ -114,9 +209,10 @@
     clipped = jnp.minimum(targets, cell_total - 1)
     state = state_start
     records = []
+    forward_x = -mixing[0]
+    forward_r = -mixing[1]
     for level in range(STEPS):
-        padded = extended(state, (("axial", 1), ("radial", 2)), 5)
-        state = advance(padded, mixing, False).at[4].add(signal[level] * forcing)
+        state = stencil_step(state, forward_x, forward_r, signal[level], forcing)
         records.append(jnp.where(live, jnp.take(state[4].reshape(-1), clipped), 0.0))
     stacked = jnp.stack(records, axis=-1)
     received = lax.all_to_all(stacked, "axial", split_axis=0, concat_axis=0, tiled=True)
@@ -142,8 +238,7 @@
         )
         carried = adjoint.at[4].add(spread.reshape(forcing.shape))
         gradient = gradient + signal[level] * carried[4]
-        padded = extended(carried, (("axial", 1), ("radial", 2)), 5)
-        adjoint = advance(padded, mixing, True)
+        adjoint = stencil_step(carried, mixing[0].T, mixing[1].T)
     return (state, mine, adjoint, gradient)
 
 

time: 1160 us -> 608 us (0.52)
  the two profiles are of different devices: /device:TPU:1 before, /device:TPU:57 now
where the time goes in v1:
time: 608 us; the launch traced here: 597 us
  starting transfers between devices  214 us (35%)
  blocking collectives  105 us (17%)
  local copies, waits for them, and re-layouts  85.2 us (14%)
  waiting for transfers between devices  71 us (12%)
  other arithmetic  53 us (9%)
  Pallas kernels  51 us (8%)
  matrix products  14.6 us (2%)
    psum x1, blocking collectives, on_device(): total = lax.psum(partial_sum, ('axial', 'radial'))  105 us
    ppermute x16, starting transfers between devices, neighbour_halos(): x_low = lax.ppermute(block[:, rows - HALO:], 'axial', up_a)  61.8 us
    ppermute x16, starting transfers between devices, neighbour_halos(): r_high = lax.ppermute(block[:, :, :HALO], 'radial', down_r)  58.6 us
    pallas_call x16, Pallas kernels, stencil_step(): pl.pallas_call(functools.partial(step_kernel, with_extra), out_shape=jax....  51 us
    ppermute x16, waiting for transfers between devices, neighbour_halos(): r_low = lax.ppermute(block[:, :, cols - HALO:], 'radial', up_r)  36 us
    ppermute x16, starting transfers between devices, neighbour_halos(): x_high = lax.ppermute(block[:, :HALO], 'axial', down_a)  34.5 us
    all_to_all x1, starting transfers between devices, on_device(): lax.all_to_all(stacked, 'axial', split_axis=0, concat_axis=0, tiled=True)  31.2 us
    unnamed x152, local copies, waits for them, and re-layouts  25.2 us
  transfers between devices with their start and end apart: 66, of which 31 were waited for; matrix products, arithmetic and copies ran while one was open for 11% of the time, Pallas kernels for 0%

profile of v1, /device:TPU:57, one launch (start us, length us, event | category | flops | bytes accessed | tf_op | source)
XLA Modules:
  0.0 596.7 jit_solution(10486409586379326660)
XLA Ops:
  5.1 3.9 collective-permute-start
  30.6 5.1 pad_maximum_fusion.8
  45.6 4.0 collective-permute-start.7
  67.8 4.0 collective-permute-start.11
  75.0 4.7 collective-permute-start.8
  90.9 4.3 collective-permute-start.15
  98.4 4.9 collective-permute-start.12
  114.3 4.3 collective-permute-start.19
  121.9 4.7 collective-permute-start.16
  137.8 4.3 collective-permute-start.23
  145.3 4.7 collective-permute-start.20
  161.2 4.3 collective-permute-start.27
  168.7 4.7 collective-permute-start.24
  184.7 5.5 collective-permute-start.31
  193.4 4.7 collective-permute-start.28
  208.5 31.2 %all-to-all-start = ((f32[64,4,8]{2,1,0:T(4,128)}), f32[64,4,8]{2,1,0:T(4,128)S(1)}, u32[]{:S(2)}, u32[]{:S(2)}) async-start(f32[64,4,8]{2,1,0:T(4,128)} %copy.66), calls=%async_computation | async-start | bytes 262144 | tf_op jit(solution)/shard_map/all_to_all | solution.py:218
  239.7 17.0 %fusion = (f32[256,4,512]{2,1,0:T(4,128)}, f32[256,4,512]{2,1,0:T(4,128)}) fusion(f32[256,512]{1,0:T(8,128)S(1)} %mul.150, f32[4]{0:T(128)S(1)} %add_multiply_fusion, f32[256,512]{1,0:T(8,128)S(1)} %mul.147, f32[256,512]{1,0:T(8,128)S(1)} %neg.29), kind=kLoop, calls=%fused_computation.20 | loop fusion | flops 1572864 | bytes 5767184 | tf_op jit(solution)/shard_map/mul | solution.py:177
  269.9 104.8 %psum.7 = f32[2,4,512]{2,1,0:T(4,128)S(1)} all-reduce(f32[2,4,512]{2,1,0:T(4,128)S(1)} %pad_maximum_fusion), channel_id=1, replica_groups=mesh['axial'=64,'radial'=8] {'axial','radial'}, use_global_device_ids=true, to_apply=%region_0.0 | all-reduce | flops 4096 | bytes 32768 | tf_op jit(solution)/shard_map/psum | solution.py:226
  382.0 7.1 %all-to-all-start.1 = ((f32[64,4,8]{2,1,0:T(4,128)}), f32[64,4,8]{2,1,0:T(4,128)S(1)}, u32[]{:S(2)}, u32[]{:S(2)}) async-start(f32[64,4,8]{2,1,0:T(4,128)} %bitcast.43), calls=%async_computation.1 | async-start | bytes 262144 | tf_op jit(solution)/shard_map/all_to_all | solution.py:229
  389.2 10.3 %all-to-all-done.1 = f32[64,4,8]{2,1,0:T(4,128)S(1)} async-done(((f32[64,4,8]{2,1,0:T(4,128)}), f32[64,4,8]{2,1,0:T(4,128)S(1)}, u32[]{:S(2)}, u32[]{:S(2)}) %all-to-all-start.1) | async-done | bytes 8224 | tf_op jit(solution)/shard_map/all_to_all | solution.py:229
  415.6 4.2 collective-permute-done.34.r_low
  431.0 3.8 collective-permute-start.39
  439.4 4.3 collective-permute-done.38.r_low
  455.0 3.9 collective-permute-start.43
  463.4 4.3 collective-permute-done.42.r_low
  479.0 3.8 collective-permute-start.47
  487.3 4.3 collective-permute-done.46.r_low
  510.1 4.3 collective-permute-done.50.r_low
  532.9 4.3 collective-permute-done.54.r_low
  555.7 4.3 collective-permute-done.58.r_low
  564.7 6.3 %bitcast_add_fusion = f32[10,16,128]{2,1,0:T(8,128)} fusion(f32[10,16,128]{2,1,0:T(8,128)S(1)} %bitcast.175, f32[]{:T(128)} %bitcast.66, f32[]{:T(128)} %bitcast.64, f32[]{:T(128)} %bitcast.62, f32[]{:T(128)} %bitcast.60, f32[]{:T(128)} %bitcast.58, f32[]{:T(128)} %bitcast.56, f32[]{:T(128)} %bitcast.54, f32[1,10,16,128]{3,2,1,0:T(8,128)S(1)} %bitcast.162, ...), kind=kLoop, calls=%fused_computation.49 | loop fusion | flops 430080 | bytes 1310748 | tf_op jit(solution)/shard_map/add | solution.py:240
  587.4 4.3 collective-permute-done.62.r_low
  (418 shorter events, 303.4 us)
Async XLA Ops:
  2.5 34.5 %collective-permute-start.1 = (f32[5,5,16,128]{3,2,1,0:T(8,128)}, f32[5,5,16,128]{3,2,1,0:T(8,128)S(1)}, u32[]{:S(2)}, u32[]{:S(2)}) collective-permute-start(f32[5,5,16,128]{3,2,1,0:T(8,128)} %get-tuple-element.184), channel_id=1, source_target_pairs={{8,0},{16,8},{24,16},{32,24},{40,32},{48,40},{56,48},{64,56},{72,6... | collective-permute-start | bytes 614408 | tf_op jit(solution)/shard_map/ppermute | solution.py:86
  5.1 32.0 %collective-permute-start = (f32[5,5,16,128]{3,2,1,0:T(8,128)}, f32[5,5,16,128]{3,2,1,0:T(8,128)}, u32[]{:S(2)}, u32[]{:S(2)}) collective-permute-start(f32[5,5,16,128]{3,2,1,0:T(8,128)} %get-tuple-element.185), channel_id=1, source_target_pairs={{0,8},{8,16},{16,24},{24,32},{32,40},{40,48},{48,56},{56,64},{64,7... | collective-permute-start | bytes 614408 | tf_op jit(solution)/shard_map/ppermute | solution.py:85
  10.8 26.2 %collective-permute-start.3 = (f32[5,10,5,128]{3,2,1,0:T(8,128)}, f32[5,10,5,128]{3,2,1,0:T(8,128)}, u32[]{:S(2)}, u32[]{:S(2)}) collective-permute-start(f32[5,10,5,128]{3,2,1,0:T(8,128)} %get-tuple-element.182), channel_id=1, source_target_pairs={{1,0},{2,1},{3,2},{4,3},{5,4},{6,5},{7,6},{9,8},{10,9},{11,10},{12... | collective-permute-start | bytes 384008 | tf_op jit(solution)/shard_map/ppermute | solution.py:88
  14.5 22.6 %collective-permute-start.2 = (f32[5,10,5,128]{3,2,1,0:T(8,128)}, f32[5,10,5,128]{3,2,1,0:T(8,128)}, u32[]{:S(2)}, u32[]{:S(2)}) collective-permute-start(f32[5,10,5,128]{3,2,1,0:T(8,128)} %get-tuple-element.183), channel_id=1, source_target_pairs={{0,1},{1,2},{2,3},{3,4},{4,5},{5,6},{6,7},{8,9},{9,10},{10,11},{11... | collective-permute-start | bytes 384008 | tf_op jit(solution)/shard_map/ppermute | solution.py:87
  45.6 10.9 %collective-permute-start.7 = (f32[5,10,5,128]{3,2,1,0:T(8,128)}, f32[5,10,5,128]{3,2,1,0:T(8,128)S(1)}, u32[]{:S(2)}, u32[]{:S(2)}) collective-permute-start(f32[5,10,5,128]{3,2,1,0:T(8,128)} %get-tuple-element.178), channel_id=1, source_target_pairs={{1,0},{2,1},{3,2},{4,3},{5,4},{6,5},{7,6},{9,8},{10,9},{11,10},{12... | collective-permute-start | bytes 384008 | tf_op jit(solution)/shard_map/ppermute | solution.py:88
  67.8 11.9 %collective-permute-start.11 = (f32[5,10,5,128]{3,2,1,0:T(8,128)}, f32[5,10,5,128]{3,2,1,0:T(8,128)S(1)}, u32[]{:S(2)}, u32[]{:S(2)}) collective-permute-start(f32[5,10,5,128]{3,2,1,0:T(8,128)} %get-tuple-element.174), channel_id=1, source_target_pairs={{1,0},{2,1},{3,2},{4,3},{5,4},{6,5},{7,6},{9,8},{10,9},{11,10},{12... | collective-permute-start | bytes 384008 | tf_op jit(solution)/shard_map/ppermute | solution.py:88
  90.9 12.4 %collective-permute-start.15 = (f32[5,10,5,128]{3,2,1,0:T(8,128)}, f32[5,10,5,128]{3,2,1,0:T(8,128)S(1)}, u32[]{:S(2)}, u32[]{:S(2)}) collective-permute-start(f32[5,10,5,128]{3,2,1,0:T(8,128)} %get-tuple-element.170), channel_id=1, source_target_pairs={{1,0},{2,1},{3,2},{4,3},{5,4},{6,5},{7,6},{9,8},{10,9},{11,10},{12... | collective-permute-start | bytes 384008 | tf_op jit(solution)/shard_map/ppermute | solution.py:88
  114.3 12.2 %collective-permute-start.19 = (f32[5,10,5,128]{3,2,1,0:T(8,128)}, f32[5,10,5,128]{3,2,1,0:T(8,128)S(1)}, u32[]{:S(2)}, u32[]{:S(2)}) collective-permute-start(f32[5,10,5,128]{3,2,1,0:T(8,128)} %get-tuple-element.166), channel_id=1, source_target_pairs={{1,0},{2,1},{3,2},{4,3},{5,4},{6,5},{7,6},{9,8},{10,9},{11,10},{12... | collective-permute-start | bytes 384008 | tf_op jit(solution)/shard_map/ppermute | solution.py:88
  137.8 12.2 %collective-permute-start.23 = (f32[5,10,5,128]{3,2,1,0:T(8,128)}, f32[5,10,5,128]{3,2,1,0:T(8,128)S(1)}, u32[]{:S(2)}, u32[]{:S(2)}) collective-permute-start(f32[5,10,5,128]{3,2,1,0:T(8,128)} %get-tuple-element.162), channel_id=1, source_target_pairs={{1,0},{2,1},{3,2},{4,3},{5,4},{6,5},{7,6},{9,8},{10,9},{11,10},{12... | collective-permute-start | bytes 384008 | tf_op jit(solution)/shard_map/ppermute | solution.py:88
  161.2 12.2 %collective-permute-start.27 = (f32[5,10,5,128]{3,2,1,0:T(8,128)}, f32[5,10,5,128]{3,2,1,0:T(8,128)S(1)}, u32[]{:S(2)}, u32[]{:S(2)}) collective-permute-start(f32[5,10,5,128]{3,2,1,0:T(8,128)} %get-tuple-element.158), channel_id=1, source_target_pairs={{1,0},{2,1},{3,2},{4,3},{5,4},{6,5},{7,6},{9,8},{10,9},{11,10},{12... | collective-permute-start | bytes 384008 | tf_op jit(solution)/shard_map/ppermute | solution.py:88
  184.7 13.4 %collective-permute-start.31 = (f32[5,10,5,128]{3,2,1,0:T(8,128)}, f32[5,10,5,128]{3,2,1,0:T(8,128)S(1)}, u32[]{:S(2)}, u32[]{:S(2)}) collective-permute-start(f32[5,10,5,128]{3,2,1,0:T(8,128)} %get-tuple-element.154), channel_id=1, source_target_pairs={{1,0},{2,1},{3,2},{4,3},{5,4},{6,5},{7,6},{9,8},{10,9},{11,10},{12... | collective-permute-start | bytes 384008 | tf_op jit(solution)/shard_map/ppermute | solution.py:88
  208.5 53.2 %all-to-all-start = ((f32[64,4,8]{2,1,0:T(4,128)}), f32[64,4,8]{2,1,0:T(4,128)S(1)}, u32[]{:S(2)}, u32[]{:S(2)}) async-start(f32[64,4,8]{2,1,0:T(4,128)} %copy.66), calls=%async_computation | async-start | bytes 262144 | tf_op jit(solution)/shard_map/all_to_all | solution.py:218
  382.0 17.5 %all-to-all-start.1 = ((f32[64,4,8]{2,1,0:T(4,128)}), f32[64,4,8]{2,1,0:T(4,128)S(1)}, u32[]{:S(2)}, u32[]{:S(2)}) async-start(f32[64,4,8]{2,1,0:T(4,128)} %bitcast.43), calls=%async_computation.1 | async-start | bytes 262144 | tf_op jit(solution)/shard_map/all_to_all | solution.py:229
  402.7 17.0 %collective-permute-start.33 = (f32[5,5,16,128]{3,2,1,0:T(8,128)S(1)}, f32[5,5,16,128]{3,2,1,0:T(8,128)S(1)}, u32[]{:S(2)}, u32[]{:S(2)}) collective-permute-start(f32[5,5,16,128]{3,2,1,0:T(8,128)S(1)} %get-tuple-element.188), channel_id=1, source_target_pairs={{8,0},{16,8},{24,16},{32,24},{40,32},{48,40},{56,48},{64,56},{72,6... | collective-permute-start | bytes 614408 | tf_op jit(solution)/shard_map/ppermute | solution.py:86
  405.0 14.7 %collective-permute-start.32 = (f32[5,5,16,128]{3,2,1,0:T(8,128)S(1)}, f32[5,5,16,128]{3,2,1,0:T(8,128)S(1)}, u32[]{:S(2)}, u32[]{:S(2)}) collective-permute-start(f32[5,5,16,128]{3,2,1,0:T(8,128)S(1)} %get-tuple-element.189), channel_id=1, source_target_pairs={{0,8},{8,16},{16,24},{24,32},{32,40},{40,48},{48,56},{56,64},{64,7... | collective-permute-start | bytes 614408 | tf_op jit(solution)/shard_map/ppermute | solution.py:85
  410.5 9.3 %collective-permute-start.34 = (f32[5,10,5,128]{3,2,1,0:T(8,128)S(1)}, f32[5,10,5,128]{3,2,1,0:T(8,128)S(1)}, u32[]{:S(2)}, u32[]{:S(2)}) collective-permute-start(f32[5,10,5,128]{3,2,1,0:T(8,128)S(1)} %get-tuple-element.187), channel_id=1, source_target_pairs={{0,1},{1,2},{2,3},{3,4},{4,5},{5,6},{6,7},{8,9},{9,10},{10,11},{11... | collective-permute-start | bytes 384008 | tf_op jit(solution)/shard_map/ppermute | solution.py:87
  425.4 18.3 %collective-permute-start.37 = (f32[5,5,16,128]{3,2,1,0:T(8,128)S(1)}, f32[5,5,16,128]{3,2,1,0:T(8,128)S(1)}, u32[]{:S(2)}, u32[]{:S(2)}) collective-permute-start(f32[5,5,16,128]{3,2,1,0:T(8,128)S(1)} %get-tuple-element.152), channel_id=1, source_target_pairs={{8,0},{16,8},{24,16},{32,24},{40,32},{48,40},{56,48},{64,56},{72,6... | collective-permute-start | bytes 614408 | tf_op jit(solution)/shard_map/ppermute | solution.py:86
  427.7 16.0 %collective-permute-start.36 = (f32[5,5,16,128]{3,2,1,0:T(8,128)S(1)}, f32[5,5,16,128]{3,2,1,0:T(8,128)S(1)}, u32[]{:S(2)}, u32[]{:S(2)}) collective-permute-start(f32[5,5,16,128]{3,2,1,0:T(8,128)S(1)} %get-tuple-element.153), channel_id=1, source_target_pairs={{0,8},{8,16},{16,24},{24,32},{32,40},{40,48},{48,56},{56,64},{64,7... | collective-permute-start | bytes 614408 | tf_op jit(solution)/shard_map/ppermute | solution.py:85
  434.9 8.8 %collective-permute-start.38 = (f32[5,10,5,128]{3,2,1,0:T(8,128)S(1)}, f32[5,10,5,128]{3,2,1,0:T(8,128)S(1)}, u32[]{:S(2)}, u32[]{:S(2)}) collective-permute-start(f32[5,10,5,128]{3,2,1,0:T(8,128)S(1)} %get-tuple-element.151), channel_id=1, source_target_pairs={{0,1},{1,2},{2,3},{3,4},{4,5},{5,6},{6,7},{8,9},{9,10},{10,11},{11... | collective-permute-start | bytes 384008 | tf_op jit(solution)/shard_map/ppermute | solution.py:87
  449.4 18.3 %collective-permute-start.41 = (f32[5,5,16,128]{3,2,1,0:T(8,128)S(1)}, f32[5,5,16,128]{3,2,1,0:T(8,128)S(1)}, u32[]{:S(2)}, u32[]{:S(2)}) collective-permute-start(f32[5,5,16,128]{3,2,1,0:T(8,128)S(1)} %get-tuple-element.148), channel_id=1, source_target_pairs={{8,0},{16,8},{24,16},{32,24},{40,32},{48,40},{56,48},{64,56},{72,6... | collective-permute-start | bytes 614408 | tf_op jit(solution)/shard_map/ppermute | solution.py:86
  451.7 16.0 %collective-permute-start.40 = (f32[5,5,16,128]{3,2,1,0:T(8,128)S(1)}, f32[5,5,16,128]{3,2,1,0:T(8,128)S(1)}, u32[]{:S(2)}, u32[]{:S(2)}) collective-permute-start(f32[5,5,16,128]{3,2,1,0:T(8,128)S(1)} %get-tuple-element.149), channel_id=1, source_target_pairs={{0,8},{8,16},{16,24},{24,32},{32,40},{40,48},{48,56},{56,64},{64,7... | collective-permute-start | bytes 614408 | tf_op jit(solution)/shard_map/ppermute | solution.py:85
  473.3 18.3 %collective-permute-start.45 = (f32[5,5,16,128]{3,2,1,0:T(8,128)S(1)}, f32[5,5,16,128]{3,2,1,0:T(8,128)S(1)}, u32[]{:S(2)}, u32[]{:S(2)}) collective-permute-start(f32[5,5,16,128]{3,2,1,0:T(8,128)S(1)} %get-tuple-element.144), channel_id=1, source_target_pairs={{8,0},{16,8},{24,16},{32,24},{40,32},{48,40},{56,48},{64,56},{72,6... | collective-permute-start | bytes 614408 | tf_op jit(solution)/shard_map/ppermute | solution.py:86
  475.7 16.0 %collective-permute-start.44 = (f32[5,5,16,128]{3,2,1,0:T(8,128)S(1)}, f32[5,5,16,128]{3,2,1,0:T(8,128)S(1)}, u32[]{:S(2)}, u32[]{:S(2)}) collective-permute-start(f32[5,5,16,128]{3,2,1,0:T(8,128)S(1)} %get-tuple-element.145), channel_id=1, source_target_pairs={{0,8},{8,16},{16,24},{24,32},{32,40},{40,48},{48,56},{56,64},{64,7... | collective-permute-start | bytes 614408 | tf_op jit(solution)/shard_map/ppermute | solution.py:85
  482.8 8.8 %collective-permute-start.46 = (f32[5,10,5,128]{3,2,1,0:T(8,128)S(1)}, f32[5,10,5,128]{3,2,1,0:T(8,128)S(1)}, u32[]{:S(2)}, u32[]{:S(2)}) collective-permute-start(f32[5,10,5,128]{3,2,1,0:T(8,128)S(1)} %get-tuple-element.143), channel_id=1, source_target_pairs={{0,1},{1,2},{2,3},{3,4},{4,5},{5,6},{6,7},{8,9},{9,10},{10,11},{11... | collective-permute-start | bytes 384008 | tf_op jit(solution)/shard_map/ppermute | solution.py:87
  497.3 17.1 %collective-permute-start.49 = (f32[5,5,16,128]{3,2,1,0:T(8,128)S(1)}, f32[5,5,16,128]{3,2,1,0:T(8,128)S(1)}, u32[]{:S(2)}, u32[]{:S(2)}) collective-permute-start(f32[5,5,16,128]{3,2,1,0:T(8,128)S(1)} %get-tuple-element.140), channel_id=1, source_target_pairs={{8,0},{16,8},{24,16},{32,24},{40,32},{48,40},{56,48},{64,56},{72,6... | collective-permute-start | bytes 614408 | tf_op jit(solution)/shard_map/ppermute | solution.py:86
  499.6 14.8 %collective-permute-start.48 = (f32[5,5,16,128]{3,2,1,0:T(8,128)S(1)}, f32[5,5,16,128]{3,2,1,0:T(8,128)S(1)}, u32[]{:S(2)}, u32[]{:S(2)}) collective-permute-start(f32[5,5,16,128]{3,2,1,0:T(8,128)S(1)} %get-tuple-element.141), channel_id=1, source_target_pairs={{0,8},{8,16},{16,24},{24,32},{32,40},{40,48},{48,56},{56,64},{64,7... | collective-permute-start | bytes 614408 | tf_op jit(solution)/shard_map/ppermute | solution.py:85
  520.1 17.1 %collective-permute-start.53 = (f32[5,5,16,128]{3,2,1,0:T(8,128)S(1)}, f32[5,5,16,128]{3,2,1,0:T(8,128)S(1)}, u32[]{:S(2)}, u32[]{:S(2)}) collective-permute-start(f32[5,5,16,128]{3,2,1,0:T(8,128)S(1)} %get-tuple-element.136), channel_id=1, source_target_pairs={{8,0},{16,8},{24,16},{32,24},{40,32},{48,40},{56,48},{64,56},{72,6... | collective-permute-start | bytes 614408 | tf_op jit(solution)/shard_map/ppermute | solution.py:86
  522.4 14.8 %collective-permute-start.52 = (f32[5,5,16,128]{3,2,1,0:T(8,128)S(1)}, f32[5,5,16,128]{3,2,1,0:T(8,128)S(1)}, u32[]{:S(2)}, u32[]{:S(2)}) collective-permute-start(f32[5,5,16,128]{3,2,1,0:T(8,128)S(1)} %get-tuple-element.137), channel_id=1, source_target_pairs={{0,8},{8,16},{16,24},{24,32},{32,40},{40,48},{48,56},{56,64},{64,7... | collective-permute-start | bytes 614408 | tf_op jit(solution)/shard_map/ppermute | solution.py:85
  543.0 17.1 %collective-permute-start.57 = (f32[5,5,16,128]{3,2,1,0:T(8,128)S(1)}, f32[5,5,16,128]{3,2,1,0:T(8,128)S(1)}, u32[]{:S(2)}, u32[]{:S(2)}) collective-permute-start(f32[5,5,16,128]{3,2,1,0:T(8,128)S(1)} %get-tuple-element.132), channel_id=1, source_target_pairs={{8,0},{16,8},{24,16},{32,24},{40,32},{48,40},{56,48},{64,56},{72,6... | collective-permute-start | bytes 614408 | tf_op jit(solution)/shard_map/ppermute | solution.py:86
  545.3 14.7 %collective-permute-start.56 = (f32[5,5,16,128]{3,2,1,0:T(8,128)S(1)}, f32[5,5,16,128]{3,2,1,0:T(8,128)S(1)}, u32[]{:S(2)}, u32[]{:S(2)}) collective-permute-start(f32[5,5,16,128]{3,2,1,0:T(8,128)S(1)} %get-tuple-element.133), channel_id=1, source_target_pairs={{0,8},{8,16},{16,24},{24,32},{32,40},{40,48},{48,56},{56,64},{64,7... | collective-permute-start | bytes 614408 | tf_op jit(solution)/shard_map/ppermute | solution.py:85
  573.6 18.1 %collective-permute-start.61 = (f32[5,5,16,128]{3,2,1,0:T(8,128)S(1)}, f32[5,5,16,128]{3,2,1,0:T(8,128)S(1)}, u32[]{:S(2)}, u32[]{:S(2)}) collective-permute-start(f32[5,5,16,128]{3,2,1,0:T(8,128)S(1)} %get-tuple-element.128), channel_id=1, source_target_pairs={{8,0},{16,8},{24,16},{32,24},{40,32},{48,40},{56,48},{64,56},{72,6... | collective-permute-start | bytes 614408 | tf_op jit(solution)/shard_map/ppermute | solution.py:86
  575.9 15.8 %collective-permute-start.60 = (f32[5,5,16,128]{3,2,1,0:T(8,128)S(1)}, f32[5,5,16,128]{3,2,1,0:T(8,128)S(1)}, u32[]{:S(2)}, u32[]{:S(2)}) collective-permute-start(f32[5,5,16,128]{3,2,1,0:T(8,128)S(1)} %get-tuple-element.129), channel_id=1, source_target_pairs={{0,8},{8,16},{16,24},{24,32},{32,40},{40,48},{48,56},{56,64},{64,7... | collective-permute-start | bytes 614408 | tf_op jit(solution)/shard_map/ppermute | solution.py:85
  (113 other events, 543.3 us)
